TPU v7x, 128 devices: a whole 4x4x4 slice. The times are simulated.
128 devices in a mesh: role: 4 (over y), section: 2 (over core), mp: 16 (over z, x).
Axes of the slice: x: 4, y: 4, z: 4, core: 2. Of those that a mesh axis runs over, the one named last changes fastest.
Arguments:
- states: bfloat16 [16, 64, 8192], P('role', None, 'mp'), may hold values from -6 to 6
- weights: bfloat16 [2, 8192, 8192], P('section', None, 'mp'), may hold values from -0.0625 to 0.0625
- head: bfloat16 [8192], P('mp'), may hold values from -0.0625 to 0.0625
- lengths: int32 [16], P('role'), may hold values from 1 to 64, as said below
- rewards: int32 [16], P('role'), may hold values from 0 to 1000
Outputs:
- weight_grads: bfloat16 [2, 8192, 8192], P('section', 'role', 'mp')
Inputs may be any that keep to these rules, and one draw needn't show every extreme that they name: `lengths`: at least one dialogue fills all 64 slots.
All inputs are finite; a program needn't handle non-finite values.
Results may differ from a plain program's by a relative error of at most 0.014.
Values may be sent and summed in bfloat16 or wider, within the bound.
A program may use at most 192 MiB of HBM per device.

v0:
```python
import jax
import jax.numpy as jnp
from jax import lax
from jax.sharding import PartitionSpec as P

MB = 4


GAMMA = 0.97


def from_behind(block, axis, distance):
    devices = range(lax.axis_size(axis))
    route = [(i - distance, i) for i in devices if i - distance in devices]
    return lax.ppermute(block, axis, route)


def silu_slope(z):
    sig = jax.nn.sigmoid(z)
    return sig * (1.0 + z * (1.0 - sig))


def targets_of(lengths, rewards, span):
    places = jnp.arange(span, dtype=jnp.int32)[None, :]
    live = places < lengths[:, None]
    mask = live.astype(jnp.float32)
    power = jnp.where(live, lengths[:, None] - 1 - places, 0).astype(jnp.float32)
    target = (
        rewards.astype(jnp.float32)[:, None] / 1000.0 * jnp.power(jnp.float32(GAMMA), power) * mask
    )
    return (target.astype(jnp.bfloat16), mask)


def per_device(states, weights, head, lengths, rewards):
    dialogs, span, width = states.shape
    target, mask = targets_of(lengths, rewards, span)
    moved, moved_target, moved_mask = (
        lax.all_to_all(states, "role", split_axis=0, concat_axis=0, tiled=True),
        lax.all_to_all(target, "role", split_axis=0, concat_axis=0, tiled=True),
        lax.all_to_all(mask.astype(jnp.bfloat16), "role", split_axis=0, concat_axis=0, tiled=True),
    )
    block_rows = dialogs * span // MB
    goals = moved_target.astype(jnp.float32)
    row_masks = moved_mask.astype(jnp.float32)
    sections = lax.axis_size("section")
    section_index = lax.axis_index("section")
    turns = MB + sections - 1
    weight = weights[0]
    model_width = weight.shape[0]
    own_width = model_width // lax.axis_size("mp")
    head_f = head.astype(jnp.float32)
    is_first = section_index == 0
    is_last = section_index == sections - 1
    received = jnp.zeros((block_rows, width), jnp.bfloat16)
    kept_inputs = []
    kept_pre = []
    kept_value = []
    for turn in range(turns):
        own_rows = moved[turn] if turn < MB else jnp.zeros_like(received)
        inputs = jnp.where(is_first, own_rows, received)
        gathered = lax.all_gather(inputs, "mp", axis=1, tiled=True)
        pre = jnp.dot(gathered, weight, preferred_element_type=jnp.float32)
        output = (inputs.astype(jnp.float32) + jax.nn.silu(pre)).astype(jnp.bfloat16)
        value = lax.psum(jnp.dot(output, head, preferred_element_type=jnp.float32), "mp")
        kept_inputs.append(inputs)
        kept_pre.append(pre)
        kept_value.append(value)
        received = from_behind(output, "section", 1)
    accum = jnp.zeros((model_width, width), jnp.float32)
    incoming = jnp.zeros((block_rows, width), jnp.bfloat16)
    for turn in range(turns):
        forward_turn = turns - 1 - turn
        micro = forward_turn - section_index
        valid = ((micro >= 0) & (micro < MB)).astype(jnp.float32)
        head_micro = forward_turn - (sections - 1)
        if 0 <= head_micro < MB:
            error = (kept_value[forward_turn] - goals[head_micro]) * row_masks[head_micro]
        else:
            error = jnp.zeros((block_rows,), jnp.float32)
        from_head = error[:, None] * head_f[None, :]
        upstream = jnp.where(is_last, from_head, incoming.astype(jnp.float32)) * valid
        slope_grad = (upstream * silu_slope(kept_pre[forward_turn])).astype(jnp.bfloat16)

        def column_grad(piece, start, slope_grad=slope_grad):
            return lax.dot_general(
                piece, slope_grad, (((0,), (0,)), ((), ())), preferred_element_type=jnp.float32
            )

        accum = accum + column_grad(
            lax.all_gather(kept_inputs[forward_turn], "mp", axis=1, tiled=True), jnp.int32(0)
        )

        def back_term(start, count, slope_grad=slope_grad):
            return lax.dot_general(
                weight, slope_grad, (((1,), (1,)), ((), ())), preferred_element_type=jnp.float32
            )

        back = lax.psum_scatter(
            back_term(jnp.int32(0), own_width * lax.axis_size("mp")).astype(jnp.bfloat16),
            "mp",
            scatter_dimension=0,
            tiled=True,
        ).astype(jnp.float32)
        passed = (upstream + back.T).astype(jnp.bfloat16)
        incoming = from_behind(passed, "section", -1)
    summed = lax.psum_scatter(accum.astype(jnp.bfloat16), "role", scatter_dimension=0, tiled=True)
    return summed[None]


def solution(mesh):
    placed = (P("role", None, "mp"), P("section", None, "mp"), P("mp"), P("role"), P("role"))
    return jax.shard_map(
        per_device,
        mesh=mesh,
        in_specs=placed,
        out_specs=P("section", "role", "mp"),
        check_vma=False,
    )
```

profile of v0, /device:TPU:16, one launch (start us, length us, event | category | flops | bytes accessed | tf_op | source)
XLA Modules:
  0.0 761.6 jit_solution(12943359962101011248)
XLA Ops:
  6.5 4.8 all-to-all-start
  11.3 3.7 all-to-all-done
  15.8 46.2 %all-gather.15.cloned.1.call-done = bf16[1,64,8192]{2,1,0:T(8,128)(2,1)} async-done(((bf16[1,64,512]{2,1,0:T(8,128)(2,1)}), bf16[1,64,8192]{2,1,0:T(8,128)(2,1)}) %all-gather.15.cloned.1.call-update) | async-done | bytes 1048592 | tf_op jit(solution)/shard_map/all_gather | solution.py:61
  61.9 5.2 fusion.21
  67.1 1.3 collective-permute-start
  68.4 0.9 collective-permute-done
  70.0 42.6 %all-gather.7.cloned.1.call-done = bf16[64,8192]{1,0:T(8,128)(2,1)} async-done(((bf16[64,512]{1,0:T(8,128)(2,1)}), bf16[64,8192]{1,0:T(8,128)(2,1)}) %all-gather.7.cloned.1.call-update) | async-done | bytes 1048592 | tf_op jit(solution)/shard_map/all_gather | solution.py:61
  112.6 5.2 add_convert_fusion.4
  117.8 1.3 collective-permute-start.1
  120.7 42.6 %all-gather.9.cloned.1.call-done = bf16[64,8192]{1,0:T(8,128)(2,1)} async-done(((bf16[64,512]{1,0:T(8,128)(2,1)}), bf16[64,8192]{1,0:T(8,128)(2,1)}) %all-gather.9.cloned.1.call-update) | async-done | bytes 1048592 | tf_op jit(solution)/shard_map/all_gather | solution.py:61
  163.4 5.2 add_convert_fusion.3
  168.6 1.3 collective-permute-start.2
  169.9 0.9 collective-permute-done.2
  171.5 42.6 %all-gather.11.cloned.1.call-done = bf16[64,8192]{1,0:T(8,128)(2,1)} async-done(((bf16[64,512]{1,0:T(8,128)(2,1)}), bf16[64,8192]{1,0:T(8,128)(2,1)}) %all-gather.11.cloned.1.call-update) | async-done | bytes 1048592 | tf_op jit(solution)/shard_map/all_gather | solution.py:61
  214.1 5.2 add_convert_fusion.2
  219.3 1.3 collective-permute-start.3
  222.8 4.8 all-to-all-start.2
  228.3 2.1 all-to-all-done.2
  230.4 5.5 all-to-all-start.1
  235.9 2.7 all-to-all-done.1
  239.0 25.7 %all-gather.13.cloned.1.call-done = bf16[64,8192]{1,0:T(8,128)(2,1)} async-done(((bf16[64,512]{1,0:T(8,128)(2,1)}), bf16[64,8192]{1,0:T(8,128)(2,1)}) %all-gather.13.cloned.1.call-update) | async-done | bytes 1048592 | tf_op jit(solution)/shard_map/all_gather | solution.py:90
  264.8 5.3 fusion.8
  270.2 38.1 %all-reduce = (f32[64]{0:T(128)S(1)}, f32[64]{0:T(128)S(1)}, f32[64]{0:T(128)S(1)}, f32[64]{0:T(128)S(1)}) all-reduce(f32[64]{0:T(128)S(1)} %convolution_bitcast_fusion.3, f32[64]{0:T(128)S(1)} %convolution_bitcast_fusion.2, f32[64]{0:T(128)S(1)} %convolution_bitcast_fusion.1, ...), channel_id=1, replica_groups=mesh['role'=4,'section'=2,'mp'=16] {'mp'}, use_global_device_ids=true, to_apply=%region_0.1 | all-reduce | flops 256 | bytes 2048 | tf_op jit(solution)/shard_map/psum | solution.py:64
  308.4 7.0 fusion
  315.4 70.4 %reduce-scatter.6.cloned.1.call-done = bf16[512,64]{0,1:T(8,128)(2,1)} async-done(((bf16[8192,64]{0,1:T(8,128)(2,1)}), bf16[512,64]{0,1:T(8,128)(2,1)}) %reduce-scatter.6.cloned.1.call-update) | async-done | bytes 65552 | tf_op jit(solution)/shard_map/reduce_scatter | solution.py:98
  385.9 0.9 fusion.25
  386.8 1.3 collective-permute-start.4
  388.1 1.8 collective-permute-done.4
  390.0 7.0 fusion.1
  397.0 73.4 %reduce-scatter.8.cloned.1.call-done = bf16[512,64]{0,1:T(8,128)(2,1)} async-done(((bf16[8192,64]{0,1:T(8,128)(2,1)}), bf16[512,64]{0,1:T(8,128)(2,1)}) %reduce-scatter.8.cloned.1.call-update) | async-done | bytes 65552 | tf_op jit(solution)/shard_map/reduce_scatter | solution.py:98
  470.4 0.9 fusion.24
  471.3 1.3 collective-permute-start.5
  472.6 1.8 collective-permute-done.5
  474.5 7.0 fusion.2
  481.6 73.5 %reduce-scatter.10.cloned.1.call-done = bf16[512,64]{0,1:T(8,128)(2,1)} async-done(((bf16[8192,64]{0,1:T(8,128)(2,1)}), bf16[512,64]{0,1:T(8,128)(2,1)}) %reduce-scatter.10.cloned.1.call-update) | async-done | bytes 65552 | tf_op jit(solution)/shard_map/reduce_scatter | solution.py:98
  555.0 0.9 fusion.23
  556.0 1.5 collective-permute-start.6
  557.5 1.7 collective-permute-done.6
  559.1 7.0 fusion.3
  566.2 8.2 %fusion.45 = f32[8192,512]{1,0:T(8,128)} fusion(bf16[64,8192]{1,0:T(8,128)(2,1)S(1)} %copy-done.3, f32[64,512]{1,0:T(8,128)S(1)} %fusion.8, f32[]{:T(128)S(6)} %convert_element_type.187, f32[512]{0:T(512)S(1)} %convert_element_type.186, f32[64]{0:T(128)S(1)} %get-tuple-element.12, pred[]{:T(512)S(6)} %eq.7), kind=kOutput, calls=%fused_computation.93 | convolution fusion | flops 537264128 | bytes 17959172 | tf_op jit(solution)/shard_map/dot_general | solution.py:85
  574.4 8.2 %fusion.46 = f32[8192,512]{1,0:T(8,128)} fusion(bf16[64,8192]{1,0:T(8,128)(2,1)S(1)} %copy-done.2, f32[64,512]{1,0:T(8,128)S(1)} %get-tuple-element.20, bf16[64,512]{1,0:T(8,128)(2,1)S(1)} %collective-permute-done.4, f32[]{:T(128)S(6)} %convert_element_type.193, f32[64]{0:T(128)S(1)} %get-tuple-element.11, f32[512]{0:T(512)S(1)} %convert_element_type.186, ...), kind=kOutput, calls=%fused_computation.94 | convolution fusion | flops 537296896 | bytes 18024708 | tf_op jit(solution)/shard_map/dot_general | solution.py:85
  582.6 8.2 %fusion.47 = f32[8192,512]{1,0:T(8,128)} fusion(bf16[64,8192]{1,0:T(8,128)(2,1)S(1)} %copy-done.1, f32[64,512]{1,0:T(8,128)S(1)} %get-tuple-element.18, bf16[64,512]{1,0:T(8,128)(2,1)S(1)} %collective-permute-done.5, f32[]{:T(128)S(6)} %convert_element_type.199, f32[64]{0:T(128)S(1)} %get-tuple-element.10, f32[512]{0:T(512)S(1)} %convert_element_type.186, ...), kind=kOutput, calls=%fused_computation.95 | convolution fusion | flops 537296896 | bytes 18024708 | tf_op jit(solution)/shard_map/dot_general | solution.py:85
  590.7 48.9 %reduce-scatter.12.cloned.1.call-done = bf16[512,64]{0,1:T(8,128)(2,1)} async-done(((bf16[8192,64]{0,1:T(8,128)(2,1)}), bf16[512,64]{0,1:T(8,128)(2,1)}) %reduce-scatter.12.cloned.1.call-update) | async-done | bytes 65552 | tf_op jit(solution)/shard_map/reduce_scatter | solution.py:98
  639.6 0.9 fusion.22
  640.6 1.6 collective-permute-start.7
  642.3 8.2 %fusion.48 = f32[8192,512]{1,0:T(8,128)} fusion(bf16[64,8192]{1,0:T(8,128)(2,1)S(1)} %copy-done, f32[64,512]{1,0:T(8,128)S(1)} %get-tuple-element.16, bf16[64,512]{1,0:T(8,128)(2,1)S(1)} %collective-permute-done.6, f32[]{:T(128)S(6)} %convert_element_type.205, f32[64]{0:T(128)S(1)} %get-tuple-element.9, f32[512]{0:T(512)S(1)} %convert_element_type.186, ...), kind=kOutput, calls=%fused_computation.96 | convolution fusion | flops 537296896 | bytes 18024708 | tf_op jit(solution)/shard_map/dot_general | solution.py:85
  650.4 25.1 %add_convert_fusion = bf16[8192,512]{1,0:T(8,128)(2,1)} fusion(f32[8192,512]{1,0:T(8,128)} %fusion.48, f32[8192,512]{1,0:T(8,128)} %fusion.47, f32[8192,512]{1,0:T(8,128)} %fusion.45, f32[8192,512]{1,0:T(8,128)} %fusion.46, f32[64,512]{1,0:T(8,128)S(1)} %get-tuple-element.14, bf16[64,512]{1,0:T(8,128)(2,1)S(1)} %collective-permute-done.7, ...), kind=kOutput, calls=%fused_computation | convolution fusion | flops 558235648 | bytes 76744712 | tf_op jit(solution)/shard_map/dot_general | solution.py:85
  675.5 79.2 %reduce-scatter.14.cloned.1.call-done = bf16[2048,512]{1,0:T(8,128)(2,1)} async-done(((bf16[8192,512]{1,0:T(8,128)(2,1)}), bf16[2048,512]{1,0:T(8,128)(2,1)}) %reduce-scatter.14.cloned.1.call-update) | async-done | bytes 2097168 | tf_op jit(solution)/shard_map/reduce_scatter | solution.py:106
  (60 shorter events, 7.4 us)
Async XLA Ops:
  6.5 8.5 %all-to-all-start = ((bf16[4,64,512]{2,1,0:T(8,128)(2,1)}), bf16[4,64,512]{2,1,0:T(8,128)(2,1)S(1)}, u32[]{:S(2)}, u32[]{:S(2)}) async-start(bf16[4,64,512]{2,1,0:T(8,128)(2,1)} %param.5), calls=%async_computation | async-start | bytes 524288 | tf_op jit(solution)/shard_map/all_to_all | solution.py:38
  11.3 50.6 %all-gather.15.cloned.1.call-start = ((), (), s32[]{:S(2)}) async-start(), calls=%async_computation.17 | async-start | bytes 1114112 | tf_op jit(solution)/shard_map/all_gather | solution.py:61
  15.7 96.9 %all-gather.7.cloned.1.call-start = ((), (), s32[]{:S(2)}) async-start(), calls=%async_computation.8 | async-start | bytes 1114112 | tf_op jit(solution)/shard_map/all_gather | solution.py:61
  67.1 2.2 collective-permute-start
  70.0 93.4 %all-gather.9.cloned.1.call-start = ((), (), s32[]{:S(2)}) async-start(), calls=%async_computation.9 | async-start | bytes 1114112 | tf_op jit(solution)/shard_map/all_gather | solution.py:61
  117.8 2.2 collective-permute-start.1
  120.7 93.4 %all-gather.11.cloned.1.call-start = ((), (), s32[]{:S(2)}) async-start(), calls=%async_computation.10 | async-start | bytes 1114112 | tf_op jit(solution)/shard_map/all_gather | solution.py:61
  168.6 2.2 collective-permute-start.2
  171.4 50.7 %copy-start.7 = (s32[4]{0:T(128)S(1)}, s32[4]{0:T(128)}, u32[]{:S(2)}) copy-start(s32[4]{0:T(128)} %param.8) | copy-start | bytes 52
  171.4 56.2 %copy-start.8 = (s32[4]{0:T(128)S(1)}, s32[4]{0:T(128)}, u32[]{:S(2)}) copy-start(s32[4]{0:T(128)} %param.9) | copy-start | bytes 52
  171.4 64.5 %copy-start.6 = (bf16[512]{0:T(512)(128)(2,1)S(1)}, bf16[512]{0:T(512)(128)(2,1)}, u32[]{:S(2)}) copy-start(bf16[512]{0:T(512)(128)(2,1)} %param.7) | copy-start | bytes 3076
  171.4 93.3 %all-gather.13.cloned.1.call-start = ((), (), s32[]{:S(2)}) async-start(), calls=%async_computation.11 | async-start | bytes 1114112 | tf_op jit(solution)/shard_map/all_gather | solution.py:90
  219.3 2.2 collective-permute-start.3
  222.8 7.6 all-to-all-start.2
  230.4 8.3 %all-to-all-start.1 = ((bf16[4,1,64]{2,1,0:T(2,128)(2,1)}), bf16[4,1,64]{2,1,0:T(2,128)(2,1)S(1)}, u32[]{:S(2)}, u32[]{:S(2)}) async-start(bf16[4,1,64]{2,1,0:T(2,128)(2,1)} %select_convert_fusion), calls=%async_computation.1 | async-start | bytes 4096 | tf_op jit(solution)/shard_map/all_to_all | solution.py:39
  235.9 150.0 %reduce-scatter.6.cloned.1.call-start = ((), (), s32[]{:S(2)}) async-start(), calls=%async_computation.12 | async-start | bytes 1114112 | tf_op jit(solution)/shard_map/reduce_scatter | solution.py:98
  239.0 31.0 %copy-start.5 = (bf16[64,512]{1,0:T(8,128)(2,1)S(1)}, bf16[64,512]{1,0:T(8,128)(2,1)}, u32[]{:S(2)}) copy-start(bf16[64,512]{1,0:T(8,128)(2,1)} %broadcast_select_fusion) | copy-start | bytes 196612
  315.4 155.0 %reduce-scatter.8.cloned.1.call-start = ((), (), s32[]{:S(2)}) async-start(), calls=%async_computation.13 | async-start | bytes 1114112 | tf_op jit(solution)/shard_map/reduce_scatter | solution.py:98
  386.8 3.1 collective-permute-start.4
  397.0 158.1 %reduce-scatter.10.cloned.1.call-start = ((), (), s32[]{:S(2)}) async-start(), calls=%async_computation.14 | async-start | bytes 1114112 | tf_op jit(solution)/shard_map/reduce_scatter | solution.py:98
  471.3 3.1 collective-permute-start.5
  481.5 84.7 %copy-start.3 = (bf16[64,8192]{1,0:T(8,128)(2,1)S(1)}, bf16[64,8192]{1,0:T(8,128)(2,1)}, u32[]{:S(2)}) copy-start(bf16[64,8192]{1,0:T(8,128)(2,1)} %all-gather.13.cloned.1.call-done) | copy-start | bytes 3145732
  481.5 158.1 %reduce-scatter.12.cloned.1.call-start = ((), (), s32[]{:S(2)}) async-start(), calls=%async_computation.15 | async-start | bytes 1114112 | tf_op jit(solution)/shard_map/reduce_scatter | solution.py:98
  556.0 3.1 collective-permute-start.6
  566.1 188.6 %reduce-scatter.14.cloned.1.call-start = ((), (), s32[]{:S(2)}) async-start(), calls=%async_computation.16 | async-start | bytes 10485760 | tf_op jit(solution)/shard_map/reduce_scatter | solution.py:106
  566.2 8.2 %copy-start.2 = (bf16[64,8192]{1,0:T(8,128)(2,1)S(1)}, bf16[64,8192]{1,0:T(8,128)(2,1)}, u32[]{:S(2)}) copy-start(bf16[64,8192]{1,0:T(8,128)(2,1)} %all-gather.11.cloned.1.call-done) | copy-start | bytes 3145732
  574.4 8.2 %copy-start.1 = (bf16[64,8192]{1,0:T(8,128)(2,1)S(1)}, bf16[64,8192]{1,0:T(8,128)(2,1)}, u32[]{:S(2)}) copy-start(bf16[64,8192]{1,0:T(8,128)(2,1)} %all-gather.9.cloned.1.call-done) | copy-start | bytes 3145732
  582.6 59.7 %copy-start = (bf16[64,8192]{1,0:T(8,128)(2,1)S(1)}, bf16[64,8192]{1,0:T(8,128)(2,1)}, u32[]{:S(2)}) copy-start(bf16[64,8192]{1,0:T(8,128)(2,1)} %all-gather.7.cloned.1.call-done) | copy-start | bytes 3145732
  640.6 9.8 %copy-start.4 = (bf16[1,64,8192]{2,1,0:T(8,128)(2,1)S(1)}, bf16[1,64,8192]{2,1,0:T(8,128)(2,1)}, u32[]{:S(2)}) copy-start(bf16[1,64,8192]{2,1,0:T(8,128)(2,1)} %all-gather.15.cloned.1.call-done) | copy-start | bytes 3145732
  640.6 9.8 %collective-permute-start.7 = (bf16[64,512]{1,0:T(8,128)(2,1)S(1)}, bf16[64,512]{1,0:T(8,128)(2,1)S(1)}, u32[]{:S(2)}, u32[]{:S(2)}) collective-permute-start(bf16[64,512]{1,0:T(8,128)(2,1)S(1)} %fusion.22), channel_id=1, source_target_pairs={{16,0},{17,1},{18,2},{19,3},{20,4},{21,5},{22,6},{23,7},{24,8},{25... | collective-permute-start | bytes 196616 | tf_op jit(solution)/shard_map/ppermute | solution.py:15
Sparse Core Ops, SparseCore 0:
  15.8 46.0 all-gather.14
  70.1 42.5 all-gather.6
  120.8 42.5 all-gather.8
  171.5 42.5 all-gather.10
  222.2 42.5 all-gather.12
  315.5 70.3 reduce-scatter.5
  397.1 73.2 reduce-scatter.7
  481.6 73.3 reduce-scatter.9
  566.3 73.3 reduce-scatter.11
  675.6 79.0 reduce-scatter.13
where the time goes:
time: 765 us; the launch traced here: 762 us
  waiting for transfers between devices  563 us (74%)
  matrix products  112 us (15%)
  blocking collectives  38.1 us (5%)
  starting transfers between devices  26.3 us (3%)
  between operations  13.8 us (2%)
  other arithmetic  8.29 us (1%)
    reduce_scatter x4, waiting for transfers between devices, per_device(): lax.psum_scatter(back_term(jnp.int32(0), own_width * lax.axis_size('mp'))...  266 us
    all_gather x4, waiting for transfers between devices, per_device(): gathered = lax.all_gather(inputs, 'mp', axis=1, tiled=True)  174 us
    reduce_scatter x1, waiting for transfers between devices, per_device(): lax.psum_scatter(accum.astype(jnp.bfloat16), 'role', scatter_dimension=0,...  79.2 us
    dot_general x5, matrix products, column_grad(): lax.dot_general(piece, slope_grad, (((0,), (0,)), ((), ())), preferred_el...  57.7 us
    psum x1, blocking collectives, per_device(): lax.psum(jnp.dot(output, head, preferred_element_type=jnp.float32), 'mp')  38.1 us
    dot_general x4, matrix products, back_term(): lax.dot_general(weight, slope_grad, (((1,), (1,)), ((), ())), preferred_e...  28 us
    dot_general x5, matrix products, per_device(): pre = jnp.dot(gathered, weight, preferred_element_type=jnp.float32)  26.1 us
    all_gather x1, waiting for transfers between devices, per_device(): lax.all_gather(kept_inputs[forward_turn], 'mp', axis=1, tiled=True)  25.7 us
  transfers between devices with their start and end apart: 21, of which 20 were waited for; matrix products, arithmetic and copies ran while one was open for 5% of the time, Pallas kernels for 0%

commit v1 on v0

v1 whole, which is shorter than its diff:
```python
import functools
import math

import jax
import jax.numpy as jnp
from jax import lax
from jax.experimental import pallas as pl
from jax.experimental.pallas import tpu as pltpu
from jax.sharding import PartitionSpec as P

MESH = pl.DeviceIdType.MESH
BF = jnp.bfloat16
F32 = jnp.float32
GAMMA = 0.97

N = 4
ROWS = 256
HALF = 128
QUART = 64
W = 512
NSEM = 200
HALVES = ((0, "x", "z"), (HALF, "z", "x"))
SIGNS = (1, -1)


def sigmoid(v):
    return 1.0 / (1.0 + jnp.exp(-v))


def kernel(states, weight, head_ref, lengths, rewards, out, wv, gath, across, relay, acc, slope,
           part, r1, r2, r3, r4, sums, dz, dzt, y1, err, vx, vz, gacc, gout,
           send_sem, recv_sem, local_sem):
    role = lax.axis_index("role")
    section = lax.axis_index("section")
    mp = lax.axis_index("mp")
    pos = {"z": mp // N, "x": mp % N}
    me = {"role": role, "section": section, "mp": mp}

    def slot(**off):
        z = lax.rem(pos["z"] + off.get("z", 0) % N, N)
        x = lax.rem(pos["x"] + off.get("x", 0) % N, N)
        return z * N + x

    def role_at(off):
        return lax.rem(role + off % N, N)

    def device(mp_index=None, role_index=None, sec=None):
        return (
            role if role_index is None else role_index,
            section if sec is None else sec,
            mp if mp_index is None else mp_index,
        )

    numbers = {}

    def number(key):
        return numbers.setdefault(key, len(numbers))

    def move(key, src, dst, dev):
        i = number(key)
        assert i < NSEM
        return pltpu.make_async_remote_copy(
            src_ref=src, dst_ref=dst, send_sem=send_sem.at[i], recv_sem=recv_sem.at[i],
            device_id=dev, device_id_type=MESH,
        )

    started = []

    def send(key, src, dst, dev):
        copy = move(key, src, dst, dev)
        copy.start()
        started.append(copy)

    def arrive(key, dst):
        move(key, dst, dst, device(mp_index=slot(x=1))).wait_recv()

    def drain():
        for copy in started:
            copy.wait_send()
        started.clear()

    def rows_of(base, sign):
        return pl.ds(base + (0 if sign > 0 else QUART), QUART)

    def gather_first(src, sec, halves=(0, 1)):
        for h in halves:
            base, f, g = HALVES[h]
            rows = pl.ds(base, HALF)
            for axis, kind in ((f, "f"), (g, "g")):
                for sg in SIGNS:
                    key = ("f", sec, h, sg) if kind == "f" else ("g", sec, h, sg, 0)
                    send(key, src.at[rows], gath.at[mp, rows], device(slot(**{axis: sg}), sec=sec))

    def gather_rest(sec, use):
        def region(h, df, dg, rows):
            _, f, g = HALVES[h]
            return gath.at[slot(**{f: df, g: dg}), rows]

        def forward(key, ref, axis, sg):
            send(key, ref, ref, device(slot(**{axis: sg})))

        for sg in SIGNS:
            for h, (base, f, g) in enumerate(HALVES):
                rows = pl.ds(base, HALF)
                block = region(h, -sg, 0, rows)
                arrive(("f", sec, h, sg), block)
                forward(("o", sec, h, sg), region(h, -sg, 0, rows_of(base, sg)), f, sg)
                for s2 in SIGNS:
                    forward(("g", sec, h, s2, sg), block, g, s2)
        for sg in SIGNS:
            for h, (base, f, g) in enumerate(HALVES):
                rows = pl.ds(base, HALF)
                arrive(("g", sec, h, sg, 0), region(h, 0, -sg, rows))
                forward(("t", sec, h, sg, 0), region(h, 0, -sg, rows_of(base, sg)), g, sg)
        for sg in SIGNS:
            for h, (base, f, g) in enumerate(HALVES):
                block = region(h, 2, 0, rows_of(base, sg))
                arrive(("o", sec, h, sg), block)
                for s2 in SIGNS:
                    forward(("g", sec, h, s2, 2 * sg), block, g, s2)
        use([(0, 0), (0, 1), (0, -1), (1, 0), (-1, 0)])
        for sf in SIGNS:
            for sg in SIGNS:
                for h, (base, f, g) in enumerate(HALVES):
                    arrive(("g", sec, h, sg, sf), region(h, -sf, -sg, pl.ds(base, HALF)))
                    forward(("t", sec, h, sg, sf), region(h, -sf, -sg, rows_of(base, sg)), g, sg)
        for sg in SIGNS:
            for h, (base, f, g) in enumerate(HALVES):
                arrive(("g", sec, h, sg, 2 * sg), region(h, 2, -sg, rows_of(base, sg)))
                forward(("t", sec, h, sg, 2), region(h, 2, -sg, rows_of(base, sg)), g, sg)
        use([(1, 1), (1, -1), (-1, 1), (-1, -1)])
        for sg in SIGNS:
            for h, (base, f, g) in enumerate(HALVES):
                arrive(("g", sec, h, sg, -2 * sg), region(h, 2, -sg, rows_of(base, -sg)))
                arrive(("t", sec, h, sg, 0), region(h, 0, 2, rows_of(base, sg)))
        use([(2, 0), (0, 2)])
        for sf in SIGNS:
            for sg in SIGNS:
                for h, (base, f, g) in enumerate(HALVES):
                    arrive(("t", sec, h, sg, sf), region(h, -sf, 2, rows_of(base, sg)))
        use([(1, 2), (-1, 2), (2, 1), (2, -1)])
        for sg in SIGNS:
            for h, (base, f, g) in enumerate(HALVES):
                arrive(("t", sec, h, sg, 2), region(h, 2, 2, rows_of(base, sg)))
        use([(2, 2)])

    def project(offsets):
        for dz_, dx_ in offsets:
            s = slot(z=dz_, x=dx_)
            add = jnp.dot(gath[s], wv[s], preferred_element_type=F32)
            if (dz_, dx_) == (0, 0):
                acc[...] = add
            else:
                acc[...] += add

    def across_first():
        for sg in SIGNS:
            far = role_at(2)
            rows = pl.ds(0 if sg > 0 else HALF, HALF)
            send(("br", sg), gath.at[pl.ds(far * N, N), rows], relay.at[0 if sg > 0 else 1],
                 device(role_index=role_at(sg)))
        for sg in SIGNS:
            to = role_at(sg)
            send(("b", sg), gath.at[pl.ds(to * N, N)], across.at[role], device(role_index=to))

    def across_relay():
        for sg in SIGNS:
            rows = pl.ds(0 if sg > 0 else HALF, HALF)
            block = relay.at[0 if sg > 0 else 1]
            arrive(("br", sg), block)
            send(("bf", sg), block, across.at[role_at(-sg), pl.ds(0, N), rows],
                 device(role_index=role_at(sg)))

    def across_last():
        for sg in SIGNS:
            arrive(("b", sg), across.at[role_at(-sg)])
        for sg in SIGNS:
            rows = pl.ds(0 if sg > 0 else HALF, HALF)
            arrive(("bf", sg), across.at[role_at(2), pl.ds(0, N), rows])

    def spread_first(src, sec, h):
        rows = pl.ds(h * HALF, HALF)
        order = (1, -1) if h == 0 else (-1, 1)
        for off in order:
            send(("d", sec, h, off), src.at[rows], dz.at[role, rows],
                 device(role_index=role_at(off), sec=sec))

    def spread_relay(sec):
        for h, sg in ((0, 1), (1, -1)):
            rows = pl.ds(h * HALF, HALF)
            block = dz.at[role_at(-sg), rows]
            arrive(("d", sec, h, sg), block)
            send(("do", sec, h), block, block, device(role_index=role_at(sg)))

    def spread_near(sec):
        for h, sg in ((0, -1), (1, 1)):
            arrive(("d", sec, h, sg), dz.at[role_at(-sg), pl.ds(h * HALF, HALF)])

    def spread_far(sec):
        for h in (0, 1):
            arrive(("do", sec, h), dz.at[role_at(2), pl.ds(h * HALF, HALF)])

    tn = (((0,), (0,)), ((), ()))

    def grads(off):
        src = role_at(off)
        for j in range(N):
            left = gath[role * N + j] if off == 0 else across[src, j]
            add = lax.dot_general(left, dz[src], tn, preferred_element_type=F32)
            if off == 0:
                gacc[j] = add
            elif off == 2:
                gout[j] = (gacc[j] + add).astype(BF)
                pltpu.make_async_copy(gout.at[j], out.at[j], local_sem.at[2 + j]).start()
            else:
                gacc[j] += add

    def grads_done():
        for j in range(N):
            pltpu.make_async_copy(gout.at[j], out.at[j], local_sem.at[2 + j]).wait()

    def by_rows(base, count, body, step=32):
        @pl.loop(0, count // step)
        def _(i):
            body(pl.ds(pl.multiple_of(base + i * step, step), step))

    load_w = pltpu.make_async_copy(weight, wv, local_sem.at[0])
    load_w.start()
    own_copy = pltpu.make_async_copy(states, gath.at[mp], local_sem.at[1])

    @pl.when(section == 0)
    def _():
        own_copy.start()

    barrier = pltpu.get_barrier_semaphore()
    peers = [device(sec=1 - section)]
    for sec in (section, 1 - section):
        peers += [device(slot(**{a: o}), sec=sec) for a in ("x", "z") for o in (1, 2, 3)]
        peers += [device(role_index=role_at(o), sec=sec) for o in (1, 2, 3)]
    for dev in peers:
        pl.semaphore_signal(barrier, inc=1, device_id=dev, device_id_type=MESH)
    pl.semaphore_wait(barrier, len(peers))

    @pl.when(section == 0)
    def _():
        gather_first(states, 0)
        own_copy.wait()
        load_w.wait()
        gather_rest(0, project)
        across_first()
        for h in (0, 1):
            def first_layer(rows):
                z = acc[rows]
                y1[rows] = (gath[mp, rows].astype(F32) + z * sigmoid(z)).astype(BF)
            by_rows(h * HALF, HALF, first_layer)
            gather_first(y1, 1, (h,))
        send(("own",), y1, gath.at[mp], device(sec=1))

        def first_slope(rows):
            z = acc[rows]
            s = sigmoid(z)
            acc[rows] = s * (1.0 + z * (1.0 - s))
        by_rows(0, ROWS, first_slope)
        send(("slope",), acc, slope, device(sec=1))
        across_relay()
        across_last()
        for h in (0, 1):
            arrive(("down", h), dz.at[role, pl.ds(h * HALF, HALF)])
        spread_relay(0)
        grads(0)
        spread_near(0)
        grads(1)
        grads(-1)
        spread_far(0)
        grads(2)
        grads_done()
        drain()

    @pl.when(section == 1)
    def _():
        load_w.wait()

        def use(offsets):
            if (0, 0) in offsets:
                arrive(("own",), gath.at[mp])
            project(offsets)

        gather_rest(1, use)
        across_first()

        head = head_ref[...]
        head_f = head.astype(F32)

        def second_layer(rows):
            z = acc[rows]
            s = sigmoid(z)
            y1[rows] = (gath[mp, rows].astype(F32) + z * s).astype(BF)
            g = head_f * (s * (1.0 + z * (1.0 - s)))
            acc[rows] = g
            dzt[rows] = g.astype(BF)
        by_rows(0, ROWS, second_layer)

        nt = (((1,), (1,)), ((), ()))
        vx[0] = lax.dot_general(jnp.broadcast_to(head, (16, W)), y1[...], nt,
                                preferred_element_type=F32)[:8]
        for o in (1, 2, 3):
            send(("vx", o), vx.at[0], vx.at[o], device(slot(x=o)))

        made = set()

        def make(z_off, x_off):
            z_off, x_off = z_off % N, x_off % N
            if (z_off, x_off) in made:
                return
            made.add((z_off, x_off))
            s = slot(z=z_off, x=x_off)
            part[s] = lax.dot_general(dzt[...], wv[s], nt, preferred_element_type=F32).astype(BF)

        def make_at(h, df, dg):
            _, f, g = HALVES[h]
            off = {f: df, g: dg}
            make(off["z"], off["x"])
            return slot(**off)

        order = (2, 1, 3, 0)
        for dg in order:
            for h, (base, f, g) in enumerate(HALVES):
                s = make_at(h, 2, dg)
                for k, sg in enumerate(SIGNS):
                    send(("r1", h, sg, dg), part.at[s, rows_of(base, sg)], r1.at[h, k, dg],
                         device(slot(**{f: sg})))
        for o in (1, 2, 3):
            arrive(("vx", o), vx.at[o])
        vz[0] = (vx[0] + vx[1]) + (vx[2] + vx[3])
        for o in (1, 2, 3):
            send(("vz", o), vz.at[0], vz.at[o], device(slot(z=o)))
        for dg in order:
            for h, (base, f, g) in enumerate(HALVES):
                for k, sg in enumerate(SIGNS):
                    s = make_at(h, sg, dg)
                    arrive(("r1", h, sg, dg), r1.at[h, k, dg])
                    rows = rows_of(base, sg)
                    part[s, rows] = (part[s, rows].astype(F32) + r1[h, k, dg].astype(F32)).astype(BF)
                    send(("r2", h, sg, dg), part.at[s, pl.ds(base, HALF)], r2.at[h, k, dg],
                         device(slot(**{f: sg})))
        make(0, 0)

        for o in (1, 2, 3):
            arrive(("vz", o), vz.at[o])
        value = (vz[0] + vz[1]) + (vz[2] + vz[3])
        lane = lax.broadcasted_iota(jnp.int32, (8, ROWS), 1)
        count = lengths.shape[0]
        span = ROWS // count
        place, which = lane % span, lane // span
        length = jnp.full((8, ROWS), lengths[0], jnp.int32)
        reward = jnp.full((8, ROWS), rewards[0], jnp.int32)
        for d in range(1, count):
            length = jnp.where(which == d, lengths[d], length)
            reward = jnp.where(which == d, rewards[d], reward)
        live = place < length
        mask = live.astype(F32)
        power = jnp.where(live, length - 1 - place, 0).astype(F32)
        target = reward.astype(F32) / 1000.0 * jnp.exp(power * math.log(GAMMA)) * mask
        error = (value - target.astype(BF).astype(F32)) * mask
        err[...] = jnp.broadcast_to(error[0:1], (128, ROWS)).T

        def second_grad(rows):
            dz[role, rows] = (err[rows][:, 0:1] * acc[rows]).astype(BF)
        by_rows(0, ROWS, second_grad)
        for h in (0, 1):
            spread_first(dz.at[role], 1, h)

        for dg in order:
            for h, (base, f, g) in enumerate(HALVES):
                s = slot(**{f: 0, g: dg})
                rows = pl.ds(base, HALF)
                for k, sg in enumerate(SIGNS):
                    arrive(("r2", h, sg, dg), r2.at[h, k, dg])
                total = part[s, rows].astype(F32) + r2[h, 0, dg].astype(F32) + r2[h, 1, dg].astype(F32)
                sums[h, dg] = total.astype(BF)
                if dg == 2:
                    for k, sg in enumerate(SIGNS):
                        send(("r3", h, sg), sums.at[h, dg, rows_of(0, sg)], r3.at[h, k],
                             device(slot(**{g: sg})))
                elif dg in (1, 3):
                    sg = 1 if dg == 1 else -1
                    k = SIGNS.index(sg)
                    arrive(("r3", h, sg), r3.at[h, k])
                    rows = rows_of(0, sg)
                    sums[h, dg, rows] = (sums[h, dg, rows].astype(F32) + r3[h, k].astype(F32)).astype(BF)
                    send(("r4", h, sg), sums.at[h, dg], r4.at[h, k], device(slot(**{g: sg})))
        arrive(("slope",), slope)
        for h, (base, f, g) in enumerate(HALVES):
            for k, sg in enumerate(SIGNS):
                arrive(("r4", h, sg), r4.at[h, k])

            @pl.loop(0, HALF // 32)
            def _(i):
                low = pl.ds(pl.multiple_of(i * 32, 32), 32)
                rows = pl.ds(pl.multiple_of(base + i * 32, 32), 32)
                back = sums[h, 0, low].astype(F32) + r4[h, 0, low].astype(F32) + r4[h, 1, low].astype(F32)
                e = err[rows][:, 0:1]
                dx = (e * head_f + e * back).astype(BF).astype(F32)
                dzt[rows] = (dx * slope[rows]).astype(BF)
            send(("down", h), dzt.at[pl.ds(base, HALF)], dz.at[role, pl.ds(base, HALF)], device(sec=0))
            spread_first(dzt, 0, h)
        across_relay()
        across_last()
        spread_relay(1)
        spread_near(1)
        spread_far(1)
        grads(0)
        grads(1)
        grads(-1)
        grads(2)
        grads_done()
        drain()


def per_device(states, weights, head, lengths, rewards):
    dialogs, span, width = states.shape
    rows = dialogs * span
    deep = weights.shape[1]
    blocks = deep // width
    dma = pltpu.SemaphoreType.DMA
    vmem = pltpu.VMEM
    out = pl.pallas_call(
        kernel,
        out_shape=jax.ShapeDtypeStruct((N, width, width), BF),
        in_specs=[
            pl.BlockSpec(memory_space=pl.ANY),
            pl.BlockSpec(memory_space=pl.ANY),
            pl.BlockSpec(memory_space=pltpu.VMEM),
            pl.BlockSpec(memory_space=pltpu.SMEM),
            pl.BlockSpec(memory_space=pltpu.SMEM),
        ],
        out_specs=pl.BlockSpec(memory_space=pl.ANY),
        scratch_shapes=[
            vmem((blocks, width, width), BF),
            vmem((blocks, rows, width), BF),
            vmem((N, N, rows, width), BF),
            vmem((2, N, HALF, width), BF),
            vmem((rows, width), F32),
            vmem((rows, width), F32),
            vmem((blocks, rows, width), BF),
            vmem((2, 2, N, QUART, width), BF),
            vmem((2, 2, N, HALF, width), BF),
            vmem((2, 2, QUART, width), BF),
            vmem((2, 2, HALF, width), BF),
            vmem((2, N, HALF, width), BF),
            vmem((N, rows, width), BF),
            vmem((rows, width), BF),
            vmem((rows, width), BF),
            vmem((rows, 128), F32),
            vmem((N, 8, rows), F32),
            vmem((N, 8, rows), F32),
            vmem((N, width, width), F32),
            vmem((N, width, width), BF),
            dma((NSEM,)),
            dma((NSEM,)),
            dma((8,)),
        ],
        compiler_params=pltpu.CompilerParams(
            collective_id=0, has_side_effects=True, vmem_limit_bytes=60 * 1024 * 1024,
        ),
        name="window_grad",
    )(
        states.reshape(rows, width),
        weights.reshape(blocks, width, width),
        head.reshape(1, width),
        lengths,
        rewards,
    )
    return out.reshape(1, N * width, width)


def solution(mesh):
    placed = (P("role", None, "mp"), P("section", None, "mp"), P("mp"), P("role"), P("role"))
    return jax.shard_map(
        per_device,
        mesh=mesh,
        in_specs=placed,
        out_specs=P("section", "role", "mp"),
        check_vma=False,
    )
```

time: 765 us -> 96.7 us (0.13)
  the two profiles are of different devices: /device:TPU:16 before, /device:TPU:1 now
where the time goes in v1:
time: 96.7 us; the launch traced here: 96.5 us
  Pallas kernels  92.2 us (95%)
  local copies, waits for them, and re-layouts  4.3 us (4%)
    pallas_call x1, Pallas kernels, per_device(): pl.pallas_call(kernel, out_shape=jax.ShapeDtypeStruct((N, width, width),...  92.2 us
    unnamed x1, local copies, waits for them, and re-layouts  3.05 us

profile of v1, /device:TPU:1, one launch (start us, length us, event | category | flops | bytes accessed | tf_op | source)
XLA Modules:
  0.0 96.5 jit_solution(17662310083526547161)
XLA Ops:
  0.0 1.3 %reshape.14.head_ref = bf16[1,512]{1,0:T(2,128)(2,1)} reshape(bf16[512]{0:T(512)(128)(2,1)} %param.7) | data formatting | bytes 2048 | tf_op jit(solution)/shard_map/reshape | solution.py:470
  1.3 92.2 %window_grad.1 = bf16[4,512,512]{2,1,0:T(8,128)(2,1)} custom-call(bf16[256,512]{1,0:T(8,128)(2,1)} %bitcast.5, bf16[16,512,512]{2,1,0:T(8,128)(2,1)} %bitcast.3, bf16[1,512]{1,0:T(2,128)(2,1)} %reshape.14.head_ref, s32[4]{0:T(128)} %lengths.1, s32[4]{0:T(128)} %rewards.1), custom_call_target="tpu_custom_call" | custom-call | tf_op jit(solution)/shard_map/window_grad/pallas_call | solution.py:427
  93.5 3.0 %copy.7 = bf16[1,2048,512]{2,1,0:T(8,128)(2,1)} copy(bf16[1,2048,512]{2,1,0:T(8,128)(2,1)} %bitcast.4) | data formatting | bytes 4194304

commit v2 on v1

--- a/solution.py
+++ b/solution.py
@@ -29,7 +29,7 @@
 
 def kernel(states, weight, head_ref, lengths, rewards, out, wv, gath, across, relay, acc, slope,
            part, r1, r2, r3, r4, sums, dz, dzt, y1, err, vx, vz, gacc, gout,
-           send_sem, recv_sem, local_sem):
+           send_sem, recv_sem, far_send, far_recv, pair_send, pair_recv, local_sem):
     role = lax.axis_index("role")
     section = lax.axis_index("section")
     mp = lax.axis_index("mp")
@@ -144,7 +144,8 @@
                 arrive(("t", sec, h, sg, 2), region(h, 2, 2, rows_of(base, sg)))
         use([(2, 2)])
 
-    def project(offsets):
+    def project(offsets, far=True):
+        across_send(offsets, far)
         for dz_, dx_ in offsets:
             s = slot(z=dz_, x=dx_)
             add = jnp.dot(gath[s], wv[s], preferred_element_type=F32)
@@ -153,52 +154,67 @@
             else:
                 acc[...] += add
 
-    def across_first():
-        for sg in SIGNS:
-            far = role_at(2)
-            rows = pl.ds(0 if sg > 0 else HALF, HALF)
-            send(("br", sg), gath.at[pl.ds(far * N, N), rows], relay.at[0 if sg > 0 else 1],
-                 device(role_index=role_at(sg)))
-        for sg in SIGNS:
-            to = role_at(sg)
-            send(("b", sg), gath.at[pl.ds(to * N, N)], across.at[role], device(role_index=to))
-
-    def across_relay():
-        for sg in SIGNS:
-            rows = pl.ds(0 if sg > 0 else HALF, HALF)
-            block = relay.at[0 if sg > 0 else 1]
-            arrive(("br", sg), block)
-            send(("bf", sg), block, across.at[role_at(-sg), pl.ds(0, N), rows],
-                 device(role_index=role_at(sg)))
-
-    def across_last():
-        for sg in SIGNS:
-            arrive(("b", sg), across.at[role_at(-sg)])
-        for sg in SIGNS:
-            rows = pl.ds(0 if sg > 0 else HALF, HALF)
-            arrive(("bf", sg), across.at[role_at(2), pl.ds(0, N), rows])
+    def across_send(offsets, far):
+        for z_off, x_off in offsets:
+            s = slot(z=z_off, x=x_off)
+            to = s // N
+
+            @pl.when(to != role if far else lax.rem(to + role, 2) == 1)
+            def _():
+                pltpu.make_async_remote_copy(
+                    src_ref=gath.at[s], dst_ref=across.at[role, lax.rem(s, N)],
+                    send_sem=far_send.at[s], recv_sem=far_recv.at[role * N + lax.rem(s, N)],
+                    device_id=device(role_index=to), device_id_type=MESH,
+                ).start()
+
+    def across_wait(off, wait):
+        other = role_at(off)
+        for j in range(N):
+            copy = pltpu.make_async_remote_copy(
+                src_ref=across.at[other, j], dst_ref=across.at[other, j],
+                send_sem=far_send.at[other * N + j], recv_sem=far_recv.at[other * N + j],
+                device_id=device(role_index=role_at(1)), device_id_type=MESH,
+            )
+            copy.wait_recv() if wait == "recv" else copy.wait_send()
+
+    line = (("x", pos["x"]), ("z", pos["z"]))
+
+    def pair_first():
+        far = role_at(2)
+        for h, (axis, at) in enumerate(line):
+            send(("pair", h), gath.at[far * N + at, pl.ds(h * HALF, HALF)], relay.at[h],
+                 device(role_index=far, sec=0))
+
+    def pair_relay():
+        for h, (axis, at) in enumerate(line):
+            arrive(("pair", h), relay.at[h])
+            for off in (2, 1, 3, 0):
+                copy = pltpu.make_async_remote_copy(
+                    src_ref=relay.at[h], dst_ref=across.at[role_at(2), at, pl.ds(h * HALF, HALF)],
+                    send_sem=pair_send.at[h, off], recv_sem=pair_recv.at[h, at],
+                    device_id=device(slot(**{axis: off}), sec=1), device_id_type=MESH,
+                )
+                copy.start()
+                started.append(copy)
+
+    def pair_wait():
+        for h in (0, 1):
+            for j in range(N):
+                block = across.at[role_at(2), j, pl.ds(h * HALF, HALF)]
+                pltpu.make_async_remote_copy(
+                    src_ref=block, dst_ref=block, send_sem=pair_send.at[h, j], recv_sem=pair_recv.at[h, j],
+                    device_id=device(sec=0), device_id_type=MESH,
+                ).wait_recv()
 
     def spread_first(src, sec, h):
         rows = pl.ds(h * HALF, HALF)
-        order = (1, -1) if h == 0 else (-1, 1)
-        for off in order:
+        for off in (2, 1, 3):
             send(("d", sec, h, off), src.at[rows], dz.at[role, rows],
                  device(role_index=role_at(off), sec=sec))
 
-    def spread_relay(sec):
-        for h, sg in ((0, 1), (1, -1)):
-            rows = pl.ds(h * HALF, HALF)
-            block = dz.at[role_at(-sg), rows]
-            arrive(("d", sec, h, sg), block)
-            send(("do", sec, h), block, block, device(role_index=role_at(sg)))
-
-    def spread_near(sec):
-        for h, sg in ((0, -1), (1, 1)):
-            arrive(("d", sec, h, sg), dz.at[role_at(-sg), pl.ds(h * HALF, HALF)])
-
-    def spread_far(sec):
+    def spread_wait(sec, off):
         for h in (0, 1):
-            arrive(("do", sec, h), dz.at[role_at(2), pl.ds(h * HALF, HALF)])
+            arrive(("d", sec, h, -off % N), dz.at[role_at(off), pl.ds(h * HALF, HALF)])
 
     tn = (((0,), (0,)), ((), ()))
 
@@ -247,7 +263,6 @@
         own_copy.wait()
         load_w.wait()
         gather_rest(0, project)
-        across_first()
         for h in (0, 1):
             def first_layer(rows):
                 z = acc[rows]
@@ -262,18 +277,17 @@
             acc[rows] = s * (1.0 + z * (1.0 - s))
         by_rows(0, ROWS, first_slope)
         send(("slope",), acc, slope, device(sec=1))
-        across_relay()
-        across_last()
+        pair_relay()
         for h in (0, 1):
             arrive(("down", h), dz.at[role, pl.ds(h * HALF, HALF)])
-        spread_relay(0)
         grads(0)
-        spread_near(0)
-        grads(1)
-        grads(-1)
-        spread_far(0)
-        grads(2)
+        for off in (1, 3, 2):
+            spread_wait(0, off)
+            across_wait(off, "recv")
+            grads(off)
         grads_done()
+        for off in (1, 2, 3):
+            across_wait(off, "send")
         drain()
 
     @pl.when(section == 1)
@@ -283,12 +297,12 @@
         def use(offsets):
             if (0, 0) in offsets:
                 arrive(("own",), gath.at[mp])
-            project(offsets)
+            project(offsets, far=False)
 
         gather_rest(1, use)
-        across_first()
-
-        head = head_ref[...]
+        pair_first()
+
+        head = head_ref[...].reshape(1, W)
         head_f = head.astype(F32)
 
         def second_layer(rows):
@@ -404,16 +418,17 @@
                 dzt[rows] = (dx * slope[rows]).astype(BF)
             send(("down", h), dzt.at[pl.ds(base, HALF)], dz.at[role, pl.ds(base, HALF)], device(sec=0))
             spread_first(dzt, 0, h)
-        across_relay()
-        across_last()
-        spread_relay(1)
-        spread_near(1)
-        spread_far(1)
         grads(0)
-        grads(1)
-        grads(-1)
-        grads(2)
+        for off in (1, 3, 2):
+            spread_wait(1, off)
+            if off == 2:
+                pair_wait()
+            else:
+                across_wait(off, "recv")
+            grads(off)
         grads_done()
+        for off in (1, 3):
+            across_wait(off, "send")
         drain()
 
 
@@ -428,8 +443,8 @@
         kernel,
         out_shape=jax.ShapeDtypeStruct((N, width, width), BF),
         in_specs=[
-            pl.BlockSpec(memory_space=pl.ANY),
-            pl.BlockSpec(memory_space=pl.ANY),
+            pl.BlockSpec(memory_space=pltpu.HBM),
+            pl.BlockSpec(memory_space=pltpu.HBM),
             pl.BlockSpec(memory_space=pltpu.VMEM),
             pl.BlockSpec(memory_space=pltpu.SMEM),
             pl.BlockSpec(memory_space=pltpu.SMEM),
@@ -439,7 +454,7 @@
             vmem((blocks, width, width), BF),
             vmem((blocks, rows, width), BF),
             vmem((N, N, rows, width), BF),
-            vmem((2, N, HALF, width), BF),
+            vmem((2, HALF, width), BF),
             vmem((rows, width), F32),
             vmem((rows, width), F32),
             vmem((blocks, rows, width), BF),
@@ -458,16 +473,20 @@
             vmem((N, width, width), BF),
             dma((NSEM,)),
             dma((NSEM,)),
+            dma((blocks,)),
+            dma((blocks,)),
+            dma((2, N)),
+            dma((2, N)),
             dma((8,)),
         ],
         compiler_params=pltpu.CompilerParams(
-            collective_id=0, has_side_effects=True, vmem_limit_bytes=60 * 1024 * 1024,
+            collective_id=0, has_side_effects=True, vmem_limit_bytes=58 * 1024 * 1024,
         ),
         name="window_grad",
     )(
         states.reshape(rows, width),
         weights.reshape(blocks, width, width),
-        head.reshape(1, width),
+        head,
         lengths,
         rewards,
     )

time: 96.7 us -> 81.4 us (0.84)
  the two profiles are of different devices: /device:TPU:1 before, /device:TPU:16 now
where the time goes in v2:
time: 81.4 us; the launch traced here: 81.3 us
  Pallas kernels  78.2 us (96%)
  local copies, waits for them, and re-layouts  3.05 us (4%)
    pallas_call x1, Pallas kernels, per_device(): pl.pallas_call(kernel, out_shape=jax.ShapeDtypeStruct((N, width, width),...  78.2 us
    unnamed x1, local copies, waits for them, and re-layouts  3.05 us

profile of v2, /device:TPU:16, one launch (start us, length us, event | category | flops | bytes accessed | tf_op | source)
XLA Modules:
  0.0 81.3 jit_solution(5723022778538211296)
XLA Ops:
  0.0 78.2 %window_grad.1 = bf16[4,512,512]{2,1,0:T(8,128)(2,1)} custom-call(bf16[256,512]{1,0:T(8,128)(2,1)} %bitcast.5, bf16[16,512,512]{2,1,0:T(8,128)(2,1)} %bitcast.3, bf16[512]{0:T(512)(128)(2,1)} %head_ref.1, s32[4]{0:T(128)} %lengths.1, s32[4]{0:T(128)} %rewards.1), custom_call_target="tpu_custom_call" | custom-call | tf_op jit(solution)/shard_map/window_grad/pallas_call | solution.py:442
  78.2 3.0 %copy.7 = bf16[1,2048,512]{2,1,0:T(8,128)(2,1)} copy(bf16[1,2048,512]{2,1,0:T(8,128)(2,1)} %bitcast.4) | data formatting | bytes 4194304

commit v3 on v2

v3 whole, which is shorter than its diff:
```python
import functools
import math

import jax
import jax.numpy as jnp
from jax import lax
from jax.experimental import pallas as pl
from jax.experimental.pallas import tpu as pltpu
from jax.sharding import PartitionSpec as P

MESH = pl.DeviceIdType.MESH
BF = jnp.bfloat16
F32 = jnp.float32
GAMMA = 0.97

N = 4
ROWS = 256
BATCH = 128
HALF = 64
QUART = 32
W = 512
NSEM = 300
HALVES = ((0, "x", "z"), (HALF, "z", "x"), (BATCH, "x", "z"), (BATCH + HALF, "z", "x"))
SIGNS = (1, -1)


def sigmoid(v):
    return 1.0 / (1.0 + jnp.exp(-v))


def kernel(states, weight, head_ref, lengths, rewards, out, wv, gath, across, relay, acc, slope,
           part, r1, r2, r3, r4, sums, dz, dzt, y1, err, vx, vz, gacc, gout,
           send_sem, recv_sem, far_send, far_recv, pair_send, pair_recv, local_sem):
    role = lax.axis_index("role")
    section = lax.axis_index("section")
    mp = lax.axis_index("mp")
    pos = {"z": mp // N, "x": mp % N}
    me = {"role": role, "section": section, "mp": mp}

    def slot(**off):
        z = lax.rem(pos["z"] + off.get("z", 0) % N, N)
        x = lax.rem(pos["x"] + off.get("x", 0) % N, N)
        return z * N + x

    def role_at(off):
        return lax.rem(role + off % N, N)

    def device(mp_index=None, role_index=None, sec=None):
        return (
            role if role_index is None else role_index,
            section if sec is None else sec,
            mp if mp_index is None else mp_index,
        )

    numbers = {}

    def number(key):
        return numbers.setdefault(key, len(numbers))

    def move(key, src, dst, dev):
        i = number(key)
        assert i < NSEM
        return pltpu.make_async_remote_copy(
            src_ref=src, dst_ref=dst, send_sem=send_sem.at[i], recv_sem=recv_sem.at[i],
            device_id=dev, device_id_type=MESH,
        )

    started = []

    def send(key, src, dst, dev):
        copy = move(key, src, dst, dev)
        copy.start()
        started.append(copy)

    def arrive(key, dst):
        move(key, dst, dst, device(mp_index=slot(x=1))).wait_recv()

    def drain():
        for copy in started:
            copy.wait_send()
        started.clear()

    def rows_of(base, sign):
        return pl.ds(base + (0 if sign > 0 else QUART), QUART)

    def halves(b):
        return [(h, HALVES[h]) for h in (2 * b, 2 * b + 1)]

    def batch(b):
        return pl.ds(b * BATCH, BATCH)

    def gather_first(src, sec, b):
        for h, _ in halves(b):
            base, f, g = HALVES[h]
            rows = pl.ds(base, HALF)
            for axis, kind in ((f, "f"), (g, "g")):
                for sg in SIGNS:
                    key = ("f", sec, h, sg) if kind == "f" else ("g", sec, h, sg, 0)
                    send(key, src.at[rows], gath.at[mp, rows], device(slot(**{axis: sg}), sec=sec))

    def gather_rest(sec, b, use):
        def region(h, df, dg, rows):
            _, f, g = HALVES[h]
            return gath.at[slot(**{f: df, g: dg}), rows]

        def forward(key, ref, axis, sg):
            send(key, ref, ref, device(slot(**{axis: sg})))

        for sg in SIGNS:
            for h, (base, f, g) in halves(b):
                rows = pl.ds(base, HALF)
                block = region(h, -sg, 0, rows)
                arrive(("f", sec, h, sg), block)
                forward(("o", sec, h, sg), region(h, -sg, 0, rows_of(base, sg)), f, sg)
                for s2 in SIGNS:
                    forward(("g", sec, h, s2, sg), block, g, s2)
        yield
        for sg in SIGNS:
            for h, (base, f, g) in halves(b):
                rows = pl.ds(base, HALF)
                arrive(("g", sec, h, sg, 0), region(h, 0, -sg, rows))
                forward(("t", sec, h, sg, 0), region(h, 0, -sg, rows_of(base, sg)), g, sg)
        yield
        for sg in SIGNS:
            for h, (base, f, g) in halves(b):
                block = region(h, 2, 0, rows_of(base, sg))
                arrive(("o", sec, h, sg), block)
                for s2 in SIGNS:
                    forward(("g", sec, h, s2, 2 * sg), block, g, s2)
        use([(0, 0), (0, 1), (0, -1), (1, 0), (-1, 0)])
        yield
        for sf in SIGNS:
            for sg in SIGNS:
                for h, (base, f, g) in halves(b):
                    arrive(("g", sec, h, sg, sf), region(h, -sf, -sg, pl.ds(base, HALF)))
                    forward(("t", sec, h, sg, sf), region(h, -sf, -sg, rows_of(base, sg)), g, sg)
        yield
        for sg in SIGNS:
            for h, (base, f, g) in halves(b):
                arrive(("g", sec, h, sg, 2 * sg), region(h, 2, -sg, rows_of(base, sg)))
                forward(("t", sec, h, sg, 2), region(h, 2, -sg, rows_of(base, sg)), g, sg)
        use([(1, 1), (1, -1), (-1, 1), (-1, -1)])
        yield
        for sg in SIGNS:
            for h, (base, f, g) in halves(b):
                arrive(("g", sec, h, sg, -2 * sg), region(h, 2, -sg, rows_of(base, -sg)))
                arrive(("t", sec, h, sg, 0), region(h, 0, 2, rows_of(base, sg)))
        use([(2, 0), (0, 2)])
        yield
        for sf in SIGNS:
            for sg in SIGNS:
                for h, (base, f, g) in halves(b):
                    arrive(("t", sec, h, sg, sf), region(h, -sf, 2, rows_of(base, sg)))
        use([(1, 2), (-1, 2), (2, 1), (2, -1)])
        yield
        for sg in SIGNS:
            for h, (base, f, g) in halves(b):
                arrive(("t", sec, h, sg, 2), region(h, 2, 2, rows_of(base, sg)))
        use([(2, 2)])

    def project(offsets, b, far=True):
        across_send(offsets, b, far)
        rows = batch(b)
        for z_off, x_off in offsets:
            s = slot(z=z_off, x=x_off)
            add = jnp.dot(gath[s, rows], wv[s], preferred_element_type=F32)
            if (z_off, x_off) == (0, 0):
                acc[rows] = add
            else:
                acc[rows] += add

    def across_send(offsets, b, far):
        for z_off, x_off in offsets:
            s = slot(z=z_off, x=x_off)
            to = s // N

            @pl.when(to != role if far else lax.rem(to + role, 2) == 1)
            def _():
                pltpu.make_async_remote_copy(
                    src_ref=gath.at[s, batch(b)], dst_ref=across.at[role, lax.rem(s, N), batch(b)],
                    send_sem=far_send.at[b, s], recv_sem=far_recv.at[b, role * N + lax.rem(s, N)],
                    device_id=device(role_index=to), device_id_type=MESH,
                ).start()

    def across_wait(off, b, wait):
        other = role_at(off)
        for j in range(N):
            copy = pltpu.make_async_remote_copy(
                src_ref=across.at[other, j, batch(b)], dst_ref=across.at[other, j, batch(b)],
                send_sem=far_send.at[b, other * N + j], recv_sem=far_recv.at[b, other * N + j],
                device_id=device(role_index=role_at(1)), device_id_type=MESH,
            )
            copy.wait_recv() if wait == "recv" else copy.wait_send()

    line = (("x", pos["x"]), ("z", pos["z"]))

    def pair_first(h):
        far = role_at(2)
        send(("pair", h), gath.at[far * N + line[h][1], batch(h)], relay.at[h],
             device(role_index=far, sec=0))

    def pair_relay():
        for h, (axis, at) in enumerate(line):
            arrive(("pair", h), relay.at[h])
            for off in (2, 1, 3, 0):
                copy = pltpu.make_async_remote_copy(
                    src_ref=relay.at[h], dst_ref=across.at[role_at(2), at, batch(h)],
                    send_sem=pair_send.at[h, off], recv_sem=pair_recv.at[h, at],
                    device_id=device(slot(**{axis: off}), sec=1), device_id_type=MESH,
                )
                copy.start()
                started.append(copy)

    def pair_wait(h):
        for j in range(N):
            block = across.at[role_at(2), j, batch(h)]
            pltpu.make_async_remote_copy(
                src_ref=block, dst_ref=block, send_sem=pair_send.at[h, j], recv_sem=pair_recv.at[h, j],
                device_id=device(sec=0), device_id_type=MESH,
            ).wait_recv()

    def spread_first(src, sec, h):
        rows = batch(h)
        for off in (2, 1, 3):
            send(("d", sec, h, off), src.at[rows], dz.at[role, rows],
                 device(role_index=role_at(off), sec=sec))

    def spread_wait(sec, off, h):
        arrive(("d", sec, h, -off % N), dz.at[role_at(off), batch(h)])

    tn = (((0,), (0,)), ((), ()))

    def grads(off, b):
        src, rows = role_at(off), batch(b)
        for j in range(N):
            left = gath[role * N + j, rows] if off == 0 else across[src, j, rows]
            add = lax.dot_general(left, dz[src, rows], tn, preferred_element_type=F32)
            if (off, b) == (0, 0):
                gacc[j] = add
            elif (off, b) == (2, 1):
                gout[j] = (gacc[j] + add).astype(BF)
                pltpu.make_async_copy(gout.at[j], out.at[j], local_sem.at[2 + j]).start()
            else:
                gacc[j] += add

    def grads_done():
        for j in range(N):
            pltpu.make_async_copy(gout.at[j], out.at[j], local_sem.at[2 + j]).wait()

    def run(steps, count=None):
        for _ in range(100 if count is None else count):
            if next(steps, steps) is steps:
                break

    def by_rows(base, count, body, step=32):
        @pl.loop(0, count // step)
        def _(i):
            body(pl.ds(pl.multiple_of(base + i * step, step), step))

    load_w = pltpu.make_async_copy(weight, wv, local_sem.at[0])
    load_w.start()
    own_copy = pltpu.make_async_copy(states, gath.at[mp], local_sem.at[1])

    @pl.when(section == 0)
    def _():
        own_copy.start()

    barrier = pltpu.get_barrier_semaphore()
    peers = [device(sec=1 - section)]
    for sec in (section, 1 - section):
        peers += [device(slot(**{a: o}), sec=sec) for a in ("x", "z") for o in (1, 2, 3)]
        peers += [device(role_index=role_at(o), sec=sec) for o in (1, 2, 3)]
    for dev in peers:
        pl.semaphore_signal(barrier, inc=1, device_id=dev, device_id_type=MESH)
    pl.semaphore_wait(barrier, len(peers))

    @pl.when(section == 0)
    def _():
        for b in (0, 1):
            gather_first(states, 0, b)
        own_copy.wait()
        load_w.wait()

        def first_layer(b):
            def body(rows):
                z = acc[rows]
                y1[rows] = (gath[mp, rows].astype(F32) + z * sigmoid(z)).astype(BF)
            for h, (base, f, g) in halves(b):
                by_rows(base, HALF, body)
            gather_first(y1, 1, b)
            send(("own", b), y1.at[batch(b)], gath.at[mp, batch(b)], device(sec=1))

        def first_slope(rows):
            z = acc[rows]
            s = sigmoid(z)
            acc[rows] = s * (1.0 + z * (1.0 - s))

        early = gather_rest(0, 0, functools.partial(project, b=0))
        late = gather_rest(0, 1, functools.partial(project, b=1))
        run(early, 3)
        for _ in range(3):
            run(late, 1)
            run(early, 1)
        run(early)
        first_layer(0)
        run(late)
        first_layer(1)
        for b in (0, 1):
            by_rows(b * BATCH, BATCH, first_slope)
            send(("slope", b), acc.at[batch(b)], slope.at[batch(b)], device(sec=1))
        pair_relay()
        for b in (0, 1):
            arrive(("down", b), dz.at[role, batch(b)])
            grads(0, b)
            for off in (1, 3, 2):
                across_wait(off, b, "recv")
                spread_wait(0, off, b)
                grads(off, b)
        grads_done()
        for b in (0, 1):
            for off in (1, 2, 3):
                across_wait(off, b, "send")
        drain()

    @pl.when(section == 1)
    def _():
        load_w.wait()

        def use(offsets, b):
            if (0, 0) in offsets:
                arrive(("own", b), gath.at[mp, batch(b)])
            project(offsets, b, far=False)

        head = head_ref[...].reshape(1, W)
        head_f = head.astype(F32)
        nt = (((1,), (1,)), ((), ()))
        order = (2, 1, 3, 0)

        def second_layer(b):
            def body(rows):
                z = acc[rows]
                s = sigmoid(z)
                y1[rows] = (gath[mp, rows].astype(F32) + z * s).astype(BF)
                g = head_f * (s * (1.0 + z * (1.0 - s)))
                acc[rows] = g
                dzt[rows] = g.astype(BF)
            by_rows(b * BATCH, BATCH, body)

        made = set()

        def make(h, df, dg):
            _, f, g = HALVES[h]
            off = {f: df % N, g: dg % N}
            s, b = slot(**off), h // 2
            key = (b, off["z"], off["x"])
            if key not in made:
                made.add(key)
                rows = batch(b)
                part[s, rows] = lax.dot_general(
                    dzt[rows], wv[s], nt, preferred_element_type=F32).astype(BF)
            return s

        def sum_far(b):
            for dg in order:
                for h, (base, f, g) in halves(b):
                    s = make(h, 2, dg)
                    for k, sg in enumerate(SIGNS):
                        send(("r1", h, sg, dg), part.at[s, rows_of(base, sg)], r1.at[h, k, dg],
                             device(slot(**{f: sg})))
                yield

        def sum_near(b):
            for dg in order:
                for h, (base, f, g) in halves(b):
                    for k, sg in enumerate(SIGNS):
                        s = make(h, sg, dg)
                        arrive(("r1", h, sg, dg), r1.at[h, k, dg])
                        rows = rows_of(base, sg)
                        part[s, rows] = (part[s, rows].astype(F32) + r1[h, k, dg].astype(F32)).astype(BF)
                        send(("r2", h, sg, dg), part.at[s, pl.ds(base, HALF)], r2.at[h, k, dg],
                             device(slot(**{f: sg})))
                yield
            make(2 * b, 0, 0)

        def sum_second(b):
            for dg in order:
                for h, (base, f, g) in halves(b):
                    s = slot(**{f: 0, g: dg})
                    rows = pl.ds(base, HALF)
                    for k, sg in enumerate(SIGNS):
                        arrive(("r2", h, sg, dg), r2.at[h, k, dg])
                    total = part[s, rows].astype(F32) + r2[h, 0, dg].astype(F32) + r2[h, 1, dg].astype(F32)
                    sums[h, dg] = total.astype(BF)
                    if dg == 2:
                        for k, sg in enumerate(SIGNS):
                            send(("r3", h, sg), sums.at[h, dg, rows_of(0, sg)], r3.at[h, k],
                                 device(slot(**{g: sg})))
                    elif dg in (1, 3):
                        sg = 1 if dg == 1 else -1
                        k = SIGNS.index(sg)
                        arrive(("r3", h, sg), r3.at[h, k])
                        rows = rows_of(0, sg)
                        sums[h, dg, rows] = (sums[h, dg, rows].astype(F32) + r3[h, k].astype(F32)).astype(BF)
                        send(("r4", h, sg), sums.at[h, dg], r4.at[h, k], device(slot(**{g: sg})))
                yield

        def finish(b):
            arrive(("slope", b), slope.at[batch(b)])
            for h, (base, f, g) in halves(b):
                for k, sg in enumerate(SIGNS):
                    arrive(("r4", h, sg), r4.at[h, k])

                @pl.loop(0, HALF // 32)
                def _(i):
                    low = pl.ds(pl.multiple_of(i * 32, 32), 32)
                    rows = pl.ds(pl.multiple_of(base + i * 32, 32), 32)
                    back = sums[h, 0, low].astype(F32) + r4[h, 0, low].astype(F32) + r4[h, 1, low].astype(F32)
                    e = err[rows][:, 0:1]
                    dx = (e * head_f + e * back).astype(BF).astype(F32)
                    dzt[rows] = (dx * slope[rows]).astype(BF)
            spread_first(dzt, 0, b)
            send(("down", b), dzt.at[batch(b)], dz.at[role, batch(b)], device(sec=0))

        run(gather_rest(1, 0, functools.partial(use, b=0)))
        pair_first(0)
        second_layer(0)
        far = sum_far(0)
        late = gather_rest(1, 1, functools.partial(use, b=1))
        for _ in range(4):
            run(late, 1)
            run(far, 1)
        run(far)
        run(late)
        pair_first(1)
        second_layer(1)
        vx[0] = lax.dot_general(jnp.broadcast_to(head, (16, W)), y1[...], nt,
                                preferred_element_type=F32)[:8]
        for o in (1, 2, 3):
            send(("vx", o), vx.at[0], vx.at[o], device(slot(x=o)))
        near, far = sum_near(0), sum_far(1)
        for _ in range(4):
            run(near, 1)
            run(far, 1)
        run(near)
        run(far)
        for o in (1, 2, 3):
            arrive(("vx", o), vx.at[o])
        vz[0] = (vx[0] + vx[1]) + (vx[2] + vx[3])
        for o in (1, 2, 3):
            send(("vz", o), vz.at[0], vz.at[o], device(slot(z=o)))
        near, second = sum_near(1), sum_second(0)
        for _ in range(4):
            run(second, 1)
            run(near, 1)
        run(second)
        run(near)

        for o in (1, 2, 3):
            arrive(("vz", o), vz.at[o])
        value = (vz[0] + vz[1]) + (vz[2] + vz[3])
        lane = lax.broadcasted_iota(jnp.int32, (8, ROWS), 1)
        count = lengths.shape[0]
        span = ROWS // count
        place, which = lane % span, lane // span
        length = jnp.full((8, ROWS), lengths[0], jnp.int32)
        reward = jnp.full((8, ROWS), rewards[0], jnp.int32)
        for d in range(1, count):
            length = jnp.where(which == d, lengths[d], length)
            reward = jnp.where(which == d, rewards[d], reward)
        live = place < length
        mask = live.astype(F32)
        power = jnp.where(live, length - 1 - place, 0).astype(F32)
        target = reward.astype(F32) / 1000.0 * jnp.exp(power * math.log(GAMMA)) * mask
        error = (value - target.astype(BF).astype(F32)) * mask
        err[...] = jnp.broadcast_to(error[0:1], (128, ROWS)).T
        finish(0)

        def second_grad(rows):
            dz[role, rows] = (err[rows][:, 0:1] * acc[rows]).astype(BF)
        by_rows(0, ROWS, second_grad)
        for b in (0, 1):
            spread_first(dz.at[role], 1, b)
        run(sum_second(1))
        finish(1)
        for b in (0, 1):
            grads(0, b)
        for off in (1, 3, 2):
            for b in (0, 1):
                spread_wait(1, off, b)
                if off == 2:
                    pair_wait(b)
                else:
                    across_wait(off, b, "recv")
                grads(off, b)
        grads_done()
        for b in (0, 1):
            for off in (1, 3):
                across_wait(off, b, "send")
        drain()


def per_device(states, weights, head, lengths, rewards):
    dialogs, span, width = states.shape
    rows = dialogs * span
    deep = weights.shape[1]
    blocks = deep // width
    dma = pltpu.SemaphoreType.DMA
    vmem = pltpu.VMEM
    out = pl.pallas_call(
        kernel,
        out_shape=jax.ShapeDtypeStruct((N, width, width), BF),
        in_specs=[
            pl.BlockSpec(memory_space=pltpu.HBM),
            pl.BlockSpec(memory_space=pltpu.HBM),
            pl.BlockSpec(memory_space=pltpu.VMEM),
            pl.BlockSpec(memory_space=pltpu.SMEM),
            pl.BlockSpec(memory_space=pltpu.SMEM),
        ],
        out_specs=pl.BlockSpec(memory_space=pl.ANY),
        scratch_shapes=[
            vmem((blocks, width, width), BF),
            vmem((blocks, rows, width), BF),
            vmem((N, N, rows, width), BF),
            vmem((2, BATCH, width), BF),
            vmem((rows, width), F32),
            vmem((rows, width), F32),
            vmem((blocks, rows, width), BF),
            vmem((4, 2, N, QUART, width), BF),
            vmem((4, 2, N, HALF, width), BF),
            vmem((4, 2, QUART, width), BF),
            vmem((4, 2, HALF, width), BF),
            vmem((4, N, HALF, width), BF),
            vmem((N, rows, width), BF),
            vmem((rows, width), BF),
            vmem((rows, width), BF),
            vmem((rows, 128), F32),
            vmem((N, 8, rows), F32),
            vmem((N, 8, rows), F32),
            vmem((N, width, width), F32),
            vmem((N, width, width), BF),
            dma((NSEM,)),
            dma((NSEM,)),
            dma((2, blocks)),
            dma((2, blocks)),
            dma((2, N)),
            dma((2, N)),
            dma((8,)),
        ],
        compiler_params=pltpu.CompilerParams(
            collective_id=0, has_side_effects=True, vmem_limit_bytes=58 * 1024 * 1024,
        ),
        name="window_grad",
    )(
        states.reshape(rows, width),
        weights.reshape(blocks, width, width),
        head,
        lengths,
        rewards,
    )
    return out.reshape(1, N * width, width)


def solution(mesh):
    placed = (P("role", None, "mp"), P("section", None, "mp"), P("mp"), P("role"), P("role"))
    return jax.shard_map(
        per_device,
        mesh=mesh,
        in_specs=placed,
        out_specs=P("section", "role", "mp"),
        check_vma=False,
    )
```

time: 81.4 us -> 88.2 us (1.084)
  Pallas kernels: 78.2 us -> 84.8 us
    pallas_call x1, Pallas kernels: 78.2 us -> 84.8 us  [per_device(): pl.pallas_call(kernel, out_shape=jax.ShapeDtypeStruct((N, width, width),...]
where the time goes in v3:
time: 88.2 us; the launch traced here: 87.8 us
  Pallas kernels  84.8 us (96%)
  local copies, waits for them, and re-layouts  3.05 us (3%)
    pallas_call x1, Pallas kernels, per_device(): pl.pallas_call(kernel, out_shape=jax.ShapeDtypeStruct((N, width, width),...  84.8 us
    unnamed x1, local copies, waits for them, and re-layouts  3.05 us

profile of v3, /device:TPU:16, one launch (start us, length us, event | category | flops | bytes accessed | tf_op | source)
XLA Modules:
  0.0 87.8 jit_solution(60195411319200586)
XLA Ops:
  0.0 84.8 %window_grad.1 = bf16[4,512,512]{2,1,0:T(8,128)(2,1)} custom-call(bf16[256,512]{1,0:T(8,128)(2,1)} %bitcast.5, bf16[16,512,512]{2,1,0:T(8,128)(2,1)} %bitcast.3, bf16[512]{0:T(512)(128)(2,1)} %head_ref.1, s32[4]{0:T(128)} %lengths.1, s32[4]{0:T(128)} %rewards.1), custom_call_target="tpu_custom_call" | custom-call | tf_op jit(solution)/shard_map/window_grad/pallas_call | solution.py:509
  84.8 3.0 %copy.7 = bf16[1,2048,512]{2,1,0:T(8,128)(2,1)} copy(bf16[1,2048,512]{2,1,0:T(8,128)(2,1)} %bitcast.4) | data formatting | bytes 4194304

commit v4 on v2

--- a/solution.py
+++ b/solution.py
@@ -348,6 +348,32 @@
         vz[0] = (vx[0] + vx[1]) + (vx[2] + vx[3])
         for o in (1, 2, 3):
             send(("vz", o), vz.at[0], vz.at[o], device(slot(z=o)))
+        def value_grad():
+            for o in (1, 2, 3):
+                arrive(("vz", o), vz.at[o])
+            value = (vz[0] + vz[1]) + (vz[2] + vz[3])
+            lane = lax.broadcasted_iota(jnp.int32, (8, ROWS), 1)
+            count = lengths.shape[0]
+            span = ROWS // count
+            place, which = lane % span, lane // span
+            length = jnp.full((8, ROWS), lengths[0], jnp.int32)
+            reward = jnp.full((8, ROWS), rewards[0], jnp.int32)
+            for d in range(1, count):
+                length = jnp.where(which == d, lengths[d], length)
+                reward = jnp.where(which == d, rewards[d], reward)
+            live = place < length
+            mask = live.astype(F32)
+            power = jnp.where(live, length - 1 - place, 0).astype(F32)
+            target = reward.astype(F32) / 1000.0 * jnp.exp(power * math.log(GAMMA)) * mask
+            error = (value - target.astype(BF).astype(F32)) * mask
+            err[...] = jnp.broadcast_to(error[0:1], (128, ROWS)).T
+
+            def second_grad(rows):
+                dz[role, rows] = (err[rows][:, 0:1] * acc[rows]).astype(BF)
+            by_rows(0, ROWS, second_grad)
+            for h in (0, 1):
+                spread_first(dz.at[role], 1, h)
+
         for dg in order:
             for h, (base, f, g) in enumerate(HALVES):
                 for k, sg in enumerate(SIGNS):
@@ -357,32 +383,9 @@
                     part[s, rows] = (part[s, rows].astype(F32) + r1[h, k, dg].astype(F32)).astype(BF)
                     send(("r2", h, sg, dg), part.at[s, pl.ds(base, HALF)], r2.at[h, k, dg],
                          device(slot(**{f: sg})))
+            if dg == 1:
+                value_grad()
         make(0, 0)
-
-        for o in (1, 2, 3):
-            arrive(("vz", o), vz.at[o])
-        value = (vz[0] + vz[1]) + (vz[2] + vz[3])
-        lane = lax.broadcasted_iota(jnp.int32, (8, ROWS), 1)
-        count = lengths.shape[0]
-        span = ROWS // count
-        place, which = lane % span, lane // span
-        length = jnp.full((8, ROWS), lengths[0], jnp.int32)
-        reward = jnp.full((8, ROWS), rewards[0], jnp.int32)
-        for d in range(1, count):
-            length = jnp.where(which == d, lengths[d], length)
-            reward = jnp.where(which == d, rewards[d], reward)
-        live = place < length
-        mask = live.astype(F32)
-        power = jnp.where(live, length - 1 - place, 0).astype(F32)
-        target = reward.astype(F32) / 1000.0 * jnp.exp(power * math.log(GAMMA)) * mask
-        error = (value - target.astype(BF).astype(F32)) * mask
-        err[...] = jnp.broadcast_to(error[0:1], (128, ROWS)).T
-
-        def second_grad(rows):
-            dz[role, rows] = (err[rows][:, 0:1] * acc[rows]).astype(BF)
-        by_rows(0, ROWS, second_grad)
-        for h in (0, 1):
-            spread_first(dz.at[role], 1, h)
 
         for dg in order:
             for h, (base, f, g) in enumerate(HALVES):

time: 81.4 us -> 81.4 us (level)
  no operation moved by 1% of the time
where the time goes in v4:
time: 81.4 us; the launch traced here: 81.3 us
  Pallas kernels  78.2 us (96%)
  local copies, waits for them, and re-layouts  3.05 us (4%)
    pallas_call x1, Pallas kernels, per_device(): pl.pallas_call(kernel, out_shape=jax.ShapeDtypeStruct((N, width, width),...  78.2 us
    unnamed x1, local copies, waits for them, and re-layouts  3.05 us

profile of v4, /device:TPU:16, one launch (start us, length us, event | category | flops | bytes accessed | tf_op | source)
XLA Modules:
  0.0 81.3 jit_solution(7762962100438442690)
XLA Ops:
  0.0 78.2 %window_grad.1 = bf16[4,512,512]{2,1,0:T(8,128)(2,1)} custom-call(bf16[256,512]{1,0:T(8,128)(2,1)} %bitcast.5, bf16[16,512,512]{2,1,0:T(8,128)(2,1)} %bitcast.3, bf16[512]{0:T(512)(128)(2,1)} %head_ref.1, s32[4]{0:T(128)} %lengths.1, s32[4]{0:T(128)} %rewards.1), custom_call_target="tpu_custom_call" | custom-call | tf_op jit(solution)/shard_map/window_grad/pallas_call | solution.py:445
  78.2 3.0 %copy.7 = bf16[1,2048,512]{2,1,0:T(8,128)(2,1)} copy(bf16[1,2048,512]{2,1,0:T(8,128)(2,1)} %bitcast.4) | data formatting | bytes 4194304
